TPU v7x, 128 devices: a whole 4x4x4 slice. The times are simulated.
128 devices in a mesh: rep: 4 (over z_lo, core), ep: 32 (over y, x, z_hi).
Axes of the slice: x: 4, y: 4, z: 4 (z_hi: 2, z_lo: 2; z = z_hi * 2 + z_lo), core: 2. Of those that a mesh axis runs over, the one named last changes fastest.
Arguments:
- tokens: bfloat16 [16384, 2048], P(('rep', 'ep')), may hold values from -6 to 6
- expert_ids: int32 [16384, 8], P(('rep', 'ep')), may hold values from 0 to 127, as said below
- route_weight: float32 [16384, 8], P(('rep', 'ep')), may hold values from 0.05 to 1
- hot_plan: int32 [32], replicated, may hold values from 0 to 3, as said below
- gate_proj: bfloat16 [128, 2048, 768], P(('rep', 'ep')), may hold values from -0.125 to 0.125
- up_proj: bfloat16 [128, 2048, 768], P(('rep', 'ep')), may hold values from -0.125 to 0.125
- down_proj: bfloat16 [128, 768, 2048], P(('rep', 'ep')), may hold values from -0.21875 to 0.21875
Outputs:
- layer_out: bfloat16 [16384, 2048], P(('rep', 'ep'))
- served_load: float32 [128], replicated
Inputs may be any that keep to these rules, and one draw needn't show every extreme that they name: `expert_ids`: within the rows of one device (aligned blocks of 128 tokens) a hot expert is named at most 16 times and any other expert at most 6 times. Some expert that is not hot is named exactly 6 times in every block, and the hot expert of some column exactly 16 times in every block. Expert hot_plan[c] * 32 + c is the hot expert of column c.
All inputs are finite; a program needn't handle non-finite values.
Results may differ from a plain program's by a relative error of at most 0.0057.
Values may be sent and summed in bfloat16 or wider, within the bound.
No kernel may reach another device: no remote copies, remote signals or barrier semaphores. Data moves between devices by JAX's collectives and lax.ppermute only.
A program may use at most 128 MiB of HBM per device.

v0:
```python
import jax
import jax.numpy as jnp
from jax import lax
from jax.sharding import PartitionSpec as P


def from_root(array, axis, root):
    mine = lax.axis_index(axis) == root
    return lax.psum(jnp.where(mine, array, jnp.zeros_like(array)), axis)


def expert_ffn(slot_rows, gate_mat, up_mat, down_mat):
    layout = slot_rows.shape
    flattened = slot_rows.reshape(-1, layout[-1])
    gate_in = jnp.dot(flattened, gate_mat, preferred_element_type=jnp.float32)
    up_in = jnp.dot(flattened, up_mat, preferred_element_type=jnp.float32)
    hidden = (jax.nn.silu(gate_in) * up_in).astype(jnp.bfloat16)
    result = jnp.dot(hidden, down_mat, preferred_element_type=jnp.float32).astype(jnp.bfloat16)
    return result.reshape(layout)


def local(tokens, expert_ids, route_weight, hot_plan, gate_proj, up_proj, down_proj):
    n_rep = lax.axis_size("rep")
    n_ep = lax.axis_size("ep")
    devices = n_rep * n_ep
    my_row = lax.axis_index("rep")
    my_col = lax.axis_index("ep")
    tok_rows, top_count = expert_ids.shape
    model_width = tokens.shape[1]
    routed = tok_rows * top_count
    cool_cap = max(2, 3 * routed // (4 * devices))
    hot_cap = max(4, 2 * routed // devices)
    flat_ids = expert_ids.reshape(-1)
    expert_range = jnp.arange(devices, dtype=jnp.int32)
    column_range = jnp.arange(n_ep, dtype=jnp.int32)
    one_hot = (flat_ids[:, None] == expert_range[None, :]).astype(jnp.int32)
    own_counts = jnp.sum(one_hot, axis=0, dtype=jnp.int32)
    row_match = (jnp.arange(n_rep, dtype=jnp.int32) == my_row)[:, None]
    placed = jnp.where(row_match, own_counts[None, :], jnp.zeros_like(own_counts)[None, :])
    row_counts = lax.psum(placed, ("rep", "ep"))
    same_column = expert_range[:, None] % n_ep == column_range[None, :]
    same_row = expert_range[:, None] // n_ep == hot_plan[None, :]
    hot_flag = jnp.any(same_column & same_row, axis=1)
    counts = jnp.sum(row_counts, axis=0, dtype=jnp.int32)
    hot_expert = hot_plan * n_ep + column_range
    copy_rows = row_counts[:, hot_expert].reshape(-1)
    served = jnp.where(hot_flag, jnp.zeros_like(counts), counts) + copy_rows
    served_load = served.astype(jnp.float32) / jnp.float32(routed)
    is_hot = jnp.sum(one_hot * hot_flag.astype(jnp.int32)[None, :], axis=1, dtype=jnp.int32) > 0
    ordinal = jnp.sum((jnp.cumsum(one_hot, axis=0) - 1) * one_hot, axis=1)
    home_col = flat_ids % n_ep
    source = jnp.arange(routed, dtype=jnp.int32) // top_count

    def pack_rows(slot, total):
        owners = jnp.zeros((total + 1,), jnp.int32).at[slot].set(source)[:total]
        filled = jnp.zeros((total + 1,), jnp.bool_).at[slot].set(True)[:total]
        return jnp.where(filled[:, None], tokens[owners], jnp.zeros((), jnp.bfloat16))

    home_total = devices * cool_cap
    home_slot = jnp.where(is_hot, home_total, flat_ids * cool_cap + ordinal)
    copy_total = n_ep * hot_cap
    copy_slot = jnp.where(is_hot, home_col * hot_cap + ordinal, copy_total)
    copy_send = pack_rows(copy_slot, copy_total).reshape(n_ep, hot_cap, model_width)
    copied = (
        from_root(gate_proj[0], "rep", hot_plan[my_col]),
        from_root(up_proj[0], "rep", hot_plan[my_col]),
        from_root(down_proj[0], "rep", hot_plan[my_col]),
    )
    copy_done = expert_ffn(
        lax.all_to_all(copy_send, "ep", split_axis=0, concat_axis=0, tiled=True),
        copied[0],
        copied[1],
        copied[2],
    )
    copy_back = lax.all_to_all(copy_done, "ep", split_axis=0, concat_axis=0, tiled=True)
    copy_result = copy_back.reshape(copy_total, model_width)[jnp.minimum(copy_slot, copy_total - 1)]
    home_send = pack_rows(home_slot, home_total).reshape(devices, cool_cap, model_width)
    home_done = expert_ffn(
        lax.all_to_all(home_send, ("rep", "ep"), split_axis=0, concat_axis=0, tiled=True),
        gate_proj[0],
        up_proj[0],
        down_proj[0],
    )
    home_back = lax.all_to_all(home_done, ("rep", "ep"), split_axis=0, concat_axis=0, tiled=True)
    home_result = home_back.reshape(home_total, model_width)[jnp.minimum(home_slot, home_total - 1)]
    gathered = jnp.where(is_hot[:, None], copy_result, home_result)
    shares = route_weight / jnp.sum(route_weight, axis=1, keepdims=True)
    combined = jnp.sum(
        shares[:, :, None] * gathered.reshape(tok_rows, top_count, model_width).astype(jnp.float32),
        axis=1,
    )
    return (combined.astype(jnp.bfloat16), served_load)


def solution(mesh):
    placed = (
        P(("rep", "ep"), None),
        P(("rep", "ep"), None),
        P(("rep", "ep"), None),
        P(),
        P(("rep", "ep"), None, None),
        P(("rep", "ep"), None, None),
        P(("rep", "ep"), None, None),
    )
    return jax.shard_map(
        local, mesh=mesh, in_specs=placed, out_specs=(P(("rep", "ep"), None), P()), check_vma=False
    )
```

profile of v0, /device:TPU:1, one launch (start us, length us, event | category | flops | bytes accessed | tf_op | source)
XLA Modules:
  0.0 456.8 jit_solution(834048434750761366)
XLA Ops:
  7.2 1.3 dynamic_slice.2
  9.2 3.9 bitcast_select_fusion.1
  13.1 1.0 copy-done.3
  14.1 3.0 bitcast_select_fusion.2
  17.2 0.7 copy-done.5
  19.4 4.3 scatter_custom_fusion.3
  23.8 4.4 gather_fusion.2
  28.1 6.3 %gather.28 = bf16[128,6,2048]{2,1,0:T(8,128)(2,1)} reshape(bf16[768,2048]{1,0:T(8,128)(2,1)} %gather_fusion.2) | data formatting | bytes 6291456 | tf_op jit(solution)/shard_map/gather | solution.py:57
  34.4 4.3 scatter_custom_fusion.2
  39.0 4.7 %broadcast_select_fusion = bf16[128,6,2048]{2,1,0:T(8,128)(2,1)} fusion(bf16[128,6,2048]{2,1,0:T(8,128)(2,1)} %gather.28, pred[128,6]{1,0:T(8,128)(4,1)S(1)} %broadcast_in_dim.123), kind=kLoop, calls=%fused_computation.11 | loop fusion | flops 1572864 | bytes 6292224 | tf_op jit(solution)/shard_map/jit(_where)/select_n | solution.py:57
  43.7 11.8 %all-to-all-start.2 = ((bf16[128,6,2048]{2,1,0:T(8,128)(2,1)}), bf16[128,6,2048]{2,1,0:T(8,128)(2,1)}, u32[]{:S(2)}, u32[]{:S(2)}) async-start(bf16[128,6,2048]{2,1,0:T(8,128)(2,1)} %broadcast_select_fusion), calls=%async_computation.2 | async-start | bytes 8388608 | tf_op jit(solution)/shard_map/all_to_all | solution.py:79
  55.6 4.5 scatter_custom_fusion.1
  60.1 4.3 scatter_custom_fusion
  64.4 2.5 gather_fusion
  67.0 1.6 broadcast_select_fusion.1
  68.6 39.2 %all-to-all-done.2 = bf16[128,6,2048]{2,1,0:T(8,128)(2,1)} async-done(((bf16[128,6,2048]{2,1,0:T(8,128)(2,1)}), bf16[128,6,2048]{2,1,0:T(8,128)(2,1)}, u32[]{:S(2)}, u32[]{:S(2)}) %all-to-all-start.2) | async-done | bytes 3145760 | tf_op jit(solution)/shard_map/all_to_all | solution.py:79
  107.8 7.8 %all-to-all-start = ((bf16[32,16,2048]{2,1,0:T(8,128)(2,1)}), bf16[32,16,2048]{2,1,0:T(8,128)(2,1)S(1)}, u32[]{:S(2)}, u32[]{:S(2)}) async-start(bf16[32,16,2048]{2,1,0:T(8,128)(2,1)} %broadcast_select_fusion.1), calls=%async_computation | async-start | bytes 4194304 | tf_op jit(solution)/shard_map/all_to_all | solution.py:70
  115.5 6.4 %reshape.314 = bf16[768,2048]{1,0:T(8,128)(2,1)} reshape(bf16[128,6,2048]{2,1,0:T(8,128)(2,1)} %all-to-all-done.2) | data formatting | bytes 6291456 | tf_op jit(solution)/shard_map/reshape | solution.py:14
  121.9 7.0 %fusion.1 = f32[768,768]{1,0:T(8,128)} fusion(bf16[768,2048]{1,0:T(8,128)(2,1)} %reshape.314, bf16[1,2048,768]{2,1,0:T(8,128)(2,1)} %param.12), kind=kOutput, calls=%fused_computation.15 | convolution fusion | flops 2415919104 | bytes 8650752 | tf_op jit(solution)/shard_map/dot_general | solution.py:16
  128.9 12.0 %convolution_convert_fusion = bf16[768,2048]{1,0:T(8,128)(2,1)} fusion(bf16[1,768,2048]{2,1,0:T(8,128)(2,1)} %param.13, f32[768,768]{1,0:T(8,128)} %fusion.1, bf16[768,2048]{1,0:T(8,128)(2,1)} %reshape.314, bf16[1,2048,768]{2,1,0:T(8,128)(2,1)} %param.11), kind=kOutput, calls=%fused_computation.12 | convolution fusion | flops 4836950016 | bytes 14942208 | tf_op jit(solution)/shard_map/dot_general | solution.py:18
  140.9 6.3 %reshape.315 = bf16[128,6,2048]{2,1,0:T(8,128)(2,1)} reshape(bf16[768,2048]{1,0:T(8,128)(2,1)} %convolution_convert_fusion) | data formatting | bytes 6291456 | tf_op jit(solution)/shard_map/reshape | solution.py:19
  147.2 10.1 %all-to-all-start.3 = ((bf16[128,6,2048]{2,1,0:T(8,128)(2,1)}), bf16[128,6,2048]{2,1,0:T(8,128)(2,1)}, u32[]{:S(2)}, u32[]{:S(2)}) async-start(bf16[128,6,2048]{2,1,0:T(8,128)(2,1)} %reshape.315), calls=%async_computation.3 | async-start | bytes 8388608 | tf_op jit(solution)/shard_map/all_to_all | solution.py:84
  157.3 153.7 %all-reduce.3.cloned.1.call-done = (bf16[768,2048]{1,0:T(8,128)(2,1)}, bf16[2048,768]{1,0:T(8,128)(2,1)}, bf16[2048,768]{1,0:T(8,128)(2,1)}) async-done(((bf16[768,2048]{1,0:T(8,128)(2,1)}, bf16[2048,768]{1,0:T(8,128)(2,1)}, bf16[2048,768]{1,0:T(8,128)(2,1)}), (bf16[768,2048]{1,0:T(8,128)(2,1)}, bf16[2048,768]{1,0:T(8,128)(2,1)}, bf16[2048,768]{1,0:T(8,128)(2,1)})) %all-reduce.3.cloned.1.call-update) | async-done | bytes 9437200 | tf_op jit(solution)/shard_map/psum | solution.py:9
  311.0 4.8 %fusion.31 = f32[512,768]{1,0:T(8,128)} fusion(bf16[512,2048]{1,0:T(8,128)(2,1)S(1)} %bitcast.52, bf16[2048,768]{1,0:T(8,128)(2,1)} %get-tuple-element.6), kind=kOutput, calls=%fused_computation.86 | convolution fusion | flops 1610612736 | bytes 6815744 | tf_op jit(solution)/shard_map/dot_general | solution.py:15
  315.8 8.6 %convolution_convert_fusion.1 = bf16[512,2048]{1,0:T(8,128)(2,1)} fusion(bf16[768,2048]{1,0:T(8,128)(2,1)} %get-tuple-element.5, f32[512,768]{1,0:T(8,128)} %fusion.31, bf16[512,2048]{1,0:T(8,128)(2,1)S(1)} %bitcast.53, bf16[2048,768]{1,0:T(8,128)(2,1)} %get-tuple-element.7), kind=kOutput, calls=%fused_computation.21 | convolution fusion | flops 3224633344 | bytes 12058624 | tf_op jit(solution)/shard_map/dot_general | solution.py:18
  324.4 9.5 %all-to-all-start.1 = ((bf16[32,16,2048]{2,1,0:T(8,128)(2,1)}), bf16[32,16,2048]{2,1,0:T(8,128)(2,1)S(1)}, u32[]{:S(2)}, u32[]{:S(2)}) async-start(bf16[32,16,2048]{2,1,0:T(8,128)(2,1)} %bitcast.51), calls=%async_computation.1 | async-start | bytes 4194304 | tf_op jit(solution)/shard_map/all_to_all | solution.py:75
  334.3 83.8 %psum.31 = s32[4,128]{0,1:T(8,128)S(1)} all-reduce(s32[4,128]{0,1:T(8,128)S(1)} %broadcast_select_fusion.2), channel_id=1, replica_groups=mesh['rep'=4,'ep'=32] {'rep','ep'}, use_global_device_ids=true, to_apply=%region_15.16 | all-reduce | flops 512 | bytes 4096 | tf_op jit(solution)/shard_map/psum | solution.py:40
  418.2 0.6 gather_fusion.4
  419.5 6.3 %reshape.316 = bf16[768,2048]{1,0:T(8,128)(2,1)} reshape(bf16[128,6,2048]{2,1,0:T(8,128)(2,1)} %all-to-all-done.3) | data formatting | bytes 6291456 | tf_op jit(solution)/shard_map/reshape | solution.py:85
  425.8 11.1 %gather_fusion.3 = bf16[1024,2048]{1,0:T(8,128)(2,1)} fusion(bf16[768,2048]{1,0:T(8,128)(2,1)} %reshape.316, s32[1024]{0:T(1024)S(1)} %broadcast_clamp_fusion), kind=kCustom, calls=%fused_computation.3 | custom fusion | bytes 8392704 | tf_op jit(solution)/shard_map/gather | solution.py:85
  437.0 6.0 %gather_fusion.1 = bf16[1024,2048]{1,0:T(8,128)(2,1)} fusion(bf16[512,2048]{1,0:T(8,128)(2,1)S(1)} %bitcast.49, s32[1024]{0:T(1024)S(1)} %broadcast_clamp_fusion.1), kind=kCustom, calls=%fused_computation.1 | custom fusion | bytes 8392704 | tf_op jit(solution)/shard_map/gather | solution.py:76
  443.0 7.0 %multiply_reduce_fusion = bf16[128,2048]{1,0:T(8,128)(2,1)} fusion(bf16[1024,2048]{1,0:T(8,128)(2,1)} %gather_fusion.3, bf16[1024,2048]{1,0:T(8,128)(2,1)} %gather_fusion.1, f32[128,8]{1,0:T(8,128)S(1)} %copy.18, pred[128,8]{1,0:T(8,128)(4,1)S(1)} %gt.32), kind=kLoop, calls=%fused_computation.9 | loop fusion | flops 8126464 | bytes 8918016 | tf_op jit(solution)/shard_map/reduce_sum | solution.py:88
  (59 shorter events, 3.0 us)
Async XLA Ops:
  7.2 16.6 %copy-start = (bf16[128,2048]{1,0:T(8,128)(2,1)S(1)}, bf16[128,2048]{1,0:T(8,128)(2,1)}, u32[]{:S(2)}) copy-start(bf16[128,2048]{1,0:T(8,128)(2,1)} %param.7) | copy-start | bytes 1572868
  7.2 303.8 %all-reduce.3.cloned.1.call-start = ((), (), s32[]{:S(2)}) async-start(), calls=%async_computation.4 | async-start | bytes 18874368 | tf_op jit(solution)/shard_map/psum | solution.py:9
  9.2 3.9 copy-start.2
  9.2 4.9 %copy-start.3 = (bf16[1,2048,768]{2,1,0:T(8,128)(2,1)S(1)}, bf16[1,2048,768]{2,1,0:T(8,128)(2,1)}, u32[]{:S(2)}) copy-start(bf16[1,2048,768]{2,1,0:T(8,128)(2,1)} %param.11) | copy-start | bytes 9437188
  17.1 0.7 copy-start.5
  17.1 1.6 copy-start.6
  43.7 64.1 %all-to-all-start.2 = ((bf16[128,6,2048]{2,1,0:T(8,128)(2,1)}), bf16[128,6,2048]{2,1,0:T(8,128)(2,1)}, u32[]{:S(2)}, u32[]{:S(2)}) async-start(bf16[128,6,2048]{2,1,0:T(8,128)(2,1)} %broadcast_select_fusion), calls=%async_computation.2 | async-start | bytes 8388608 | tf_op jit(solution)/shard_map/all_to_all | solution.py:79
  107.8 39.4 %all-to-all-start = ((bf16[32,16,2048]{2,1,0:T(8,128)(2,1)}), bf16[32,16,2048]{2,1,0:T(8,128)(2,1)S(1)}, u32[]{:S(2)}, u32[]{:S(2)}) async-start(bf16[32,16,2048]{2,1,0:T(8,128)(2,1)} %broadcast_select_fusion.1), calls=%async_computation | async-start | bytes 4194304 | tf_op jit(solution)/shard_map/all_to_all | solution.py:70
  147.2 177.3 %all-to-all-start.3 = ((bf16[128,6,2048]{2,1,0:T(8,128)(2,1)}), bf16[128,6,2048]{2,1,0:T(8,128)(2,1)}, u32[]{:S(2)}, u32[]{:S(2)}) async-start(bf16[128,6,2048]{2,1,0:T(8,128)(2,1)} %reshape.315), calls=%async_computation.3 | async-start | bytes 8388608 | tf_op jit(solution)/shard_map/all_to_all | solution.py:84
  324.4 9.6 %copy-start.4 = (f32[128,8]{0,1:T(8,128)S(1)}, f32[128,8]{0,1:T(8,128)}, u32[]{:S(2)}) copy-start(f32[128,8]{0,1:T(8,128)} %param.9) | copy-start | bytes 12292
  324.4 112.5 %all-to-all-start.1 = ((bf16[32,16,2048]{2,1,0:T(8,128)(2,1)}), bf16[32,16,2048]{2,1,0:T(8,128)(2,1)S(1)}, u32[]{:S(2)}, u32[]{:S(2)}) async-start(bf16[32,16,2048]{2,1,0:T(8,128)(2,1)} %bitcast.51), calls=%async_computation.1 | async-start | bytes 4194304 | tf_op jit(solution)/shard_map/all_to_all | solution.py:75
  436.9 13.0 %copy-start.1 = (bf16[128,2048]{1,0:T(8,128)(2,1)S(1)}, bf16[128,2048]{1,0:T(8,128)(2,1)}, u32[]{:S(2)}) copy-start(bf16[128,2048]{1,0:T(8,128)(2,1)} %param.7) | copy-start | bytes 1572868
Sparse Core Ops, SparseCore 0:
  17.3 293.6 all-reduce.2
where the time goes:
time: 458 us; the launch traced here: 457 us
  waiting for transfers between devices  193 us (42%)
  blocking collectives  83.8 us (18%)
  local copies, waits for them, and re-layouts  71.5 us (16%)
  starting transfers between devices  39.2 us (9%)
  matrix products  32.5 us (7%)
  other arithmetic  21.9 us (5%)
  between operations  15 us (3%)
    psum x1, waiting for transfers between devices, from_root(): return lax.psum(jnp.where(mine, array, jnp.zeros_like(array)), axis)  154 us
    psum x1, blocking collectives, local(): row_counts = lax.psum(placed, ('rep', 'ep'))  83.8 us
    all_to_all x1, waiting for transfers between devices, local(): lax.all_to_all(home_send, ('rep', 'ep'), split_axis=0, concat_axis=0, til...  39.2 us
    dot_general x2, matrix products, expert_ffn(): jnp.dot(hidden, down_mat, preferred_element_type=jnp.float32)  20.7 us
    gather x3, local copies, waits for them, and re-layouts, pack_rows(): tokens[owners]  13.1 us
    all_to_all x1, starting transfers between devices, local(): lax.all_to_all(home_send, ('rep', 'ep'), split_axis=0, concat_axis=0, til...  11.8 us
    gather x1, local copies, waits for them, and re-layouts, local(): home_back.reshape(home_total, model_width)  11.1 us
    all_to_all x1, starting transfers between devices, local(): lax.all_to_all(home_done, ('rep', 'ep'), split_axis=0, concat_axis=0, til...  10.1 us
  transfers between devices with their start and end apart: 5, of which 2 were waited for; matrix products, arithmetic and copies ran while one was open for 23% of the time, Pallas kernels for 0%

commit v1 on v0

--- a/solution.py
+++ b/solution.py
@@ -2,6 +2,11 @@
 import jax.numpy as jnp
 from jax import lax
 from jax.sharding import PartitionSpec as P
+
+
+def by_each_axis(value, first, second):
+    half = lax.psum(value, first)
+    return lax.psum(half, second)
 
 
 def from_root(array, axis, root):
@@ -37,7 +42,7 @@
     own_counts = jnp.sum(one_hot, axis=0, dtype=jnp.int32)
     row_match = (jnp.arange(n_rep, dtype=jnp.int32) == my_row)[:, None]
     placed = jnp.where(row_match, own_counts[None, :], jnp.zeros_like(own_counts)[None, :])
-    row_counts = lax.psum(placed, ("rep", "ep"))
+    row_counts = by_each_axis(placed, "rep", "ep")
     same_column = expert_range[:, None] % n_ep == column_range[None, :]
     same_row = expert_range[:, None] // n_ep == hot_plan[None, :]
     hot_flag = jnp.any(same_column & same_row, axis=1)

time: 458 us -> 587 us (1.28)
  the two profiles are of different devices: /device:TPU:1 before, /device:TPU:0 now
where the time goes in v1:
time: 587 us; the launch traced here: 586 us
  blocking collectives  214 us (36%)
  waiting for transfers between devices  191 us (33%)
  local copies, waits for them, and re-layouts  71.6 us (12%)
  starting transfers between devices  40.4 us (7%)
  matrix products  32.4 us (6%)
  other arithmetic  21.9 us (4%)
  between operations  15 us (3%)
    psum x1, blocking collectives, by_each_axis(): return lax.psum(half, second)  186 us
    psum x1, waiting for transfers between devices, from_root(): return lax.psum(jnp.where(mine, array, jnp.zeros_like(array)), axis)  153 us
    all_to_all x1, waiting for transfers between devices, local(): lax.all_to_all(home_send, ('rep', 'ep'), split_axis=0, concat_axis=0, til...  38 us
    psum x1, blocking collectives, by_each_axis(): half = lax.psum(value, first)  27.9 us
    dot_general x2, matrix products, expert_ffn(): jnp.dot(hidden, down_mat, preferred_element_type=jnp.float32)  20.6 us
    gather x3, local copies, waits for them, and re-layouts, pack_rows(): tokens[owners]  13.2 us
  transfers between devices with their start and end apart: 5, of which 2 were waited for; matrix products, arithmetic and copies ran while one was open for 18% of the time, Pallas kernels for 0%

profile of v1, /device:TPU:0, one launch (start us, length us, event | category | flops | bytes accessed | tf_op | source)
XLA Modules:
  0.0 585.5 jit_solution(13967426779845397310)
XLA Ops:
  7.2 1.3 dynamic_slice.2
  9.2 3.9 bitcast_select_fusion.1
  13.1 1.0 copy-done.3
  14.1 3.0 bitcast_select_fusion.2
  17.2 0.7 copy-done.5
  19.4 4.3 scatter_custom_fusion.3
  23.8 4.4 gather_fusion.2
  28.1 6.4 %gather.28 = bf16[128,6,2048]{2,1,0:T(8,128)(2,1)} reshape(bf16[768,2048]{1,0:T(8,128)(2,1)} %gather_fusion.2) | data formatting | bytes 6291456 | tf_op jit(solution)/shard_map/gather | solution.py:62
  34.5 4.3 scatter_custom_fusion.2
  39.0 4.7 broadcast_select_fusion
  43.7 11.6 %all-to-all-start.2 = ((bf16[128,6,2048]{2,1,0:T(8,128)(2,1)}), bf16[128,6,2048]{2,1,0:T(8,128)(2,1)}, u32[]{:S(2)}, u32[]{:S(2)}) async-start(bf16[128,6,2048]{2,1,0:T(8,128)(2,1)} %broadcast_select_fusion), calls=%async_computation.2 | async-start | bytes 8388608 | tf_op jit(solution)/shard_map/all_to_all | solution.py:84
  55.3 4.5 scatter_custom_fusion.1
  59.8 4.3 scatter_custom_fusion
  64.2 2.5 gather_fusion
  66.8 1.6 broadcast_select_fusion.1
  68.3 38.0 %all-to-all-done.2 = bf16[128,6,2048]{2,1,0:T(8,128)(2,1)} async-done(((bf16[128,6,2048]{2,1,0:T(8,128)(2,1)}), bf16[128,6,2048]{2,1,0:T(8,128)(2,1)}, u32[]{:S(2)}, u32[]{:S(2)}) %all-to-all-start.2) | async-done | bytes 3145760 | tf_op jit(solution)/shard_map/all_to_all | solution.py:84
  106.3 8.5 %all-to-all-start = ((bf16[32,16,2048]{2,1,0:T(8,128)(2,1)}), bf16[32,16,2048]{2,1,0:T(8,128)(2,1)S(1)}, u32[]{:S(2)}, u32[]{:S(2)}) async-start(bf16[32,16,2048]{2,1,0:T(8,128)(2,1)} %broadcast_select_fusion.1), calls=%async_computation | async-start | bytes 4194304 | tf_op jit(solution)/shard_map/all_to_all | solution.py:75
  114.9 6.4 %reshape.314 = bf16[768,2048]{1,0:T(8,128)(2,1)} reshape(bf16[128,6,2048]{2,1,0:T(8,128)(2,1)} %all-to-all-done.2) | data formatting | bytes 6291456 | tf_op jit(solution)/shard_map/reshape | solution.py:19
  121.2 7.0 %fusion.1 = f32[768,768]{1,0:T(8,128)} fusion(bf16[768,2048]{1,0:T(8,128)(2,1)} %reshape.314, bf16[1,2048,768]{2,1,0:T(8,128)(2,1)} %param.12), kind=kOutput, calls=%fused_computation.15 | convolution fusion | flops 2415919104 | bytes 8650752 | tf_op jit(solution)/shard_map/dot_general | solution.py:21
  128.2 12.0 %convolution_convert_fusion = bf16[768,2048]{1,0:T(8,128)(2,1)} fusion(bf16[1,768,2048]{2,1,0:T(8,128)(2,1)} %param.13, f32[768,768]{1,0:T(8,128)} %fusion.1, bf16[768,2048]{1,0:T(8,128)(2,1)} %reshape.314, bf16[1,2048,768]{2,1,0:T(8,128)(2,1)} %param.11), kind=kOutput, calls=%fused_computation.12 | convolution fusion | flops 4836950016 | bytes 14942208 | tf_op jit(solution)/shard_map/dot_general | solution.py:23
  140.2 6.3 %reshape.315 = bf16[128,6,2048]{2,1,0:T(8,128)(2,1)} reshape(bf16[768,2048]{1,0:T(8,128)(2,1)} %convolution_convert_fusion) | data formatting | bytes 6291456 | tf_op jit(solution)/shard_map/reshape | solution.py:24
  146.5 10.5 %all-to-all-start.3 = ((bf16[128,6,2048]{2,1,0:T(8,128)(2,1)}), bf16[128,6,2048]{2,1,0:T(8,128)(2,1)}, u32[]{:S(2)}, u32[]{:S(2)}) async-start(bf16[128,6,2048]{2,1,0:T(8,128)(2,1)} %reshape.315), calls=%async_computation.3 | async-start | bytes 8388608 | tf_op jit(solution)/shard_map/all_to_all | solution.py:89
  157.0 152.7 %all-reduce.3.cloned.1.call-done = (bf16[768,2048]{1,0:T(8,128)(2,1)}, bf16[2048,768]{1,0:T(8,128)(2,1)}, bf16[2048,768]{1,0:T(8,128)(2,1)}) async-done(((bf16[768,2048]{1,0:T(8,128)(2,1)}, bf16[2048,768]{1,0:T(8,128)(2,1)}, bf16[2048,768]{1,0:T(8,128)(2,1)}), (bf16[768,2048]{1,0:T(8,128)(2,1)}, bf16[2048,768]{1,0:T(8,128)(2,1)}, bf16[2048,768]{1,0:T(8,128)(2,1)})) %all-reduce.3.cloned.1.call-update) | async-done | bytes 9437200 | tf_op jit(solution)/shard_map/psum | solution.py:14
  309.7 4.8 fusion.31
  314.5 8.6 %convolution_convert_fusion.1 = bf16[512,2048]{1,0:T(8,128)(2,1)} fusion(bf16[768,2048]{1,0:T(8,128)(2,1)} %get-tuple-element.5, f32[512,768]{1,0:T(8,128)} %fusion.31, bf16[512,2048]{1,0:T(8,128)(2,1)S(1)} %bitcast.53, bf16[2048,768]{1,0:T(8,128)(2,1)} %get-tuple-element.7), kind=kOutput, calls=%fused_computation.21 | convolution fusion | flops 3224633344 | bytes 12058624 | tf_op jit(solution)/shard_map/dot_general | solution.py:23
  323.2 9.7 %all-to-all-start.1 = ((bf16[32,16,2048]{2,1,0:T(8,128)(2,1)}), bf16[32,16,2048]{2,1,0:T(8,128)(2,1)S(1)}, u32[]{:S(2)}, u32[]{:S(2)}) async-start(bf16[32,16,2048]{2,1,0:T(8,128)(2,1)} %bitcast.51), calls=%async_computation.1 | async-start | bytes 4194304 | tf_op jit(solution)/shard_map/all_to_all | solution.py:80
  333.2 27.9 %psum.38 = s32[4,128]{0,1:T(8,128)S(1)} all-reduce(s32[4,128]{0,1:T(8,128)S(1)} %broadcast_select_fusion.2), channel_id=1, replica_groups=mesh['rep'=4,'ep'=32] {'rep'}, use_global_device_ids=true, to_apply=%region_15.16 | all-reduce | flops 512 | bytes 4096 | tf_op jit(solution)/shard_map/psum | solution.py:8
  361.1 185.7 %psum.39 = s32[4,128]{0,1:T(8,128)S(1)} all-reduce(s32[4,128]{0,1:T(8,128)S(1)} %psum.38), channel_id=1, replica_groups=mesh['rep'=4,'ep'=32] {'ep'}, use_global_device_ids=true, to_apply=%region_16.17 | all-reduce | flops 512 | bytes 4096 | tf_op jit(solution)/shard_map/psum | solution.py:9
  548.2 6.3 %reshape.316 = bf16[768,2048]{1,0:T(8,128)(2,1)} reshape(bf16[128,6,2048]{2,1,0:T(8,128)(2,1)} %all-to-all-done.3) | data formatting | bytes 6291456 | tf_op jit(solution)/shard_map/reshape | solution.py:90
  554.5 11.1 %gather_fusion.3 = bf16[1024,2048]{1,0:T(8,128)(2,1)} fusion(bf16[768,2048]{1,0:T(8,128)(2,1)} %reshape.316, s32[1024]{0:T(1024)S(1)} %broadcast_clamp_fusion), kind=kCustom, calls=%fused_computation.3 | custom fusion | bytes 8392704 | tf_op jit(solution)/shard_map/gather | solution.py:90
  565.7 6.0 %gather_fusion.1 = bf16[1024,2048]{1,0:T(8,128)(2,1)} fusion(bf16[512,2048]{1,0:T(8,128)(2,1)S(1)} %bitcast.49, s32[1024]{0:T(1024)S(1)} %broadcast_clamp_fusion.1), kind=kCustom, calls=%fused_computation.1 | custom fusion | bytes 8392704 | tf_op jit(solution)/shard_map/gather | solution.py:81
  571.7 7.0 %multiply_reduce_fusion = bf16[128,2048]{1,0:T(8,128)(2,1)} fusion(bf16[1024,2048]{1,0:T(8,128)(2,1)} %gather_fusion.3, bf16[1024,2048]{1,0:T(8,128)(2,1)} %gather_fusion.1, f32[128,8]{1,0:T(8,128)S(1)} %copy.18, pred[128,8]{1,0:T(8,128)(4,1)S(1)} %gt.32), kind=kLoop, calls=%fused_computation.9 | loop fusion | flops 8126464 | bytes 8918016 | tf_op jit(solution)/shard_map/reduce_sum | solution.py:93
  (60 shorter events, 3.6 us)
Async XLA Ops:
  7.2 16.6 %copy-start = (bf16[128,2048]{1,0:T(8,128)(2,1)S(1)}, bf16[128,2048]{1,0:T(8,128)(2,1)}, u32[]{:S(2)}) copy-start(bf16[128,2048]{1,0:T(8,128)(2,1)} %param.7) | copy-start | bytes 1572868
  7.2 302.5 %all-reduce.3.cloned.1.call-start = ((), (), s32[]{:S(2)}) async-start(), calls=%async_computation.4 | async-start | bytes 18874368 | tf_op jit(solution)/shard_map/psum | solution.py:14
  9.2 3.9 copy-start.2
  9.2 4.9 copy-start.3
  17.1 0.7 copy-start.5
  17.1 1.6 copy-start.6
  43.7 62.6 %all-to-all-start.2 = ((bf16[128,6,2048]{2,1,0:T(8,128)(2,1)}), bf16[128,6,2048]{2,1,0:T(8,128)(2,1)}, u32[]{:S(2)}, u32[]{:S(2)}) async-start(bf16[128,6,2048]{2,1,0:T(8,128)(2,1)} %broadcast_select_fusion), calls=%async_computation.2 | async-start | bytes 8388608 | tf_op jit(solution)/shard_map/all_to_all | solution.py:84
  106.3 40.2 %all-to-all-start = ((bf16[32,16,2048]{2,1,0:T(8,128)(2,1)}), bf16[32,16,2048]{2,1,0:T(8,128)(2,1)S(1)}, u32[]{:S(2)}, u32[]{:S(2)}) async-start(bf16[32,16,2048]{2,1,0:T(8,128)(2,1)} %broadcast_select_fusion.1), calls=%async_computation | async-start | bytes 4194304 | tf_op jit(solution)/shard_map/all_to_all | solution.py:75
  146.5 176.7 %all-to-all-start.3 = ((bf16[128,6,2048]{2,1,0:T(8,128)(2,1)}), bf16[128,6,2048]{2,1,0:T(8,128)(2,1)}, u32[]{:S(2)}, u32[]{:S(2)}) async-start(bf16[128,6,2048]{2,1,0:T(8,128)(2,1)} %reshape.315), calls=%async_computation.3 | async-start | bytes 8388608 | tf_op jit(solution)/shard_map/all_to_all | solution.py:89
  323.1 9.9 %copy-start.4 = (f32[128,8]{0,1:T(8,128)S(1)}, f32[128,8]{0,1:T(8,128)}, u32[]{:S(2)}) copy-start(f32[128,8]{0,1:T(8,128)} %param.9) | copy-start | bytes 12292
  323.2 242.5 %all-to-all-start.1 = ((bf16[32,16,2048]{2,1,0:T(8,128)(2,1)}), bf16[32,16,2048]{2,1,0:T(8,128)(2,1)S(1)}, u32[]{:S(2)}, u32[]{:S(2)}) async-start(bf16[32,16,2048]{2,1,0:T(8,128)(2,1)} %bitcast.51), calls=%async_computation.1 | async-start | bytes 4194304 | tf_op jit(solution)/shard_map/all_to_all | solution.py:80
  565.6 13.0 %copy-start.1 = (bf16[128,2048]{1,0:T(8,128)(2,1)S(1)}, bf16[128,2048]{1,0:T(8,128)(2,1)}, u32[]{:S(2)}) copy-start(bf16[128,2048]{1,0:T(8,128)(2,1)} %param.7) | copy-start | bytes 1572868
Sparse Core Ops, SparseCore 0:
  17.3 292.3 all-reduce.2
